TPU v7x, 32 devices: a whole 2x2x4 slice. The times are simulated.
32 devices in a mesh: cond: 4 (over y, x), space: 8 (over z, core).
Axes of the slice: x: 2, y: 2, z: 4, core: 2. Of those that a mesh axis runs over, the one named last changes fastest.
Arguments:
- flow: float32 [8, 3, 128, 2048], P('cond', None, 'space'), may hold values from -4 to 4
- forcing: float32 [8, 2, 128, 2048], P('cond', None, 'space'), may hold values from -4 to 4
- wet: int32 [8, 128, 2048], P('cond', 'space'), may hold values 0 or 1
- depth: float32 [128, 2048], P('space'), may hold values from 0.5 to 2
- limiter: int32 [128, 2048], P('space'), may hold values 0 or 1
- weights: int32 [8], replicated, may hold values from 1 to 9
- bed: float32 [128, 2048], P('space'), may hold values from -6 to 6
- diffusivity: float32 [128, 2048], P('space'), may hold values from 0.2 to 5
Outputs:
- surface: float32 [8, 128, 2048], P('cond', 'space')
- bed_new: float32 [128, 2048], P('space')
All inputs are finite; a program needn't handle non-finite values. No bound on the sum of `wet` or of `limiter` on one device may be relied on, other than what follows from the above.
Results may differ from a plain program's by a relative error of at most 0.0001.
Values sent between devices are 32-bit elements; how exact they have to be, the bound alone decides.
No kernel may reach another device: no remote copies, remote signals or barrier semaphores. Data moves between devices by JAX's collectives and lax.ppermute only.
A program may use at most 64 MiB of HBM per device.

v0:
```python
import jax
import jax.numpy as jnp
from jax import lax
from jax.sharding import PartitionSpec as P

STEPS = 4
ITERS = 2
time_step = 0.4
gravity = 1.0
friction = 0.1
transport_base = 0.5
morph_factor = 1.0
slope_coeff = 1.0


def with_halo(cells, sides, width):
    for axis, dim in sides:
        count = lax.axis_size(axis)
        ends = count - 1
        head = lax.slice_in_dim(cells, 0, width, axis=dim)
        tail = lax.slice_in_dim(cells, cells.shape[dim] - width, cells.shape[dim], axis=dim)
        cells = jnp.concatenate(
            [
                lax.ppermute(tail, axis, [(i, (i + 1) % count) for i in range(ends)]),
                cells,
                lax.ppermute(head, axis, [((i + 1) % count, i) for i in range(ends)]),
            ],
            axis=dim,
        )
    return cells


def rows_diff(padded):
    return 0.5 * (padded[..., 2:, :] - padded[..., :-2, :])


def column_diff(field):
    padded = jnp.pad(field, [(0, 0)] * (field.ndim - 1) + [(1, 1)])
    return 0.5 * (padded[..., 2:] - padded[..., :-2])


def paired_fields(state_now, depth):
    return [state_now[:, 0], depth * state_now[:, 1]]


def flow_rim(state_now, depth):
    paired = jnp.stack(paired_fields(state_now, depth), 1)
    return with_halo(paired, (("space", 2),), 1)


def tendency(state_now, rim_rows, depth, wet_mask, force):
    elevation, vel_first, vel_second = (state_now[:, 0], state_now[:, 1], state_now[:, 2])
    rate_elev = -(rows_diff(rim_rows[:, 1]) + column_diff(depth * vel_second))
    rate_first = -gravity * rows_diff(rim_rows[:, 0]) - friction * vel_first + force[:, 0]
    rate_second = -gravity * column_diff(elevation) - friction * vel_second + force[:, 1]
    return wet_mask * jnp.stack([rate_elev, rate_first, rate_second], 1)


def transport(state_now, limit_mask):
    vel_first, vel_second = (state_now[:, 1], state_now[:, 2])
    energy = vel_first * vel_first + vel_second * vel_second
    factor = (transport_base + energy) / (1.0 + limit_mask * energy)
    return (vel_first * factor, vel_second * factor)


def second_section(state_now, rim_rows, depth, wet_mask, forcing):
    first_section = state_now + time_step * tendency(state_now, rim_rows, depth, wet_mask, forcing)
    rim_next = flow_rim(first_section, depth)
    return 0.5 * (
        state_now
        + first_section
        + time_step * tendency(first_section, rim_next, depth, wet_mask, forcing)
    )


def rim_cells(field):
    padded = with_halo(field, (("space", 0),), 1)
    return jnp.pad(padded, ((0, 0), (1, 1)))


def reduce_all(values):
    return lax.psum(values, "space")


def neighbours(padded):
    return [padded[:-2, 1:-1], padded[2:, 1:-1], padded[1:-1, :-2], padded[1:-1, 2:]]


def apply_op(field, coefs):
    near = neighbours(rim_cells(field))
    total = coefs[0] * (field - near[0]) + coefs[1] * (field - near[1])
    total = total + coefs[2] * (field - near[2]) + coefs[3] * (field - near[3])
    return field + slope_coeff * total


def local(flow, forcing, wet, depth, limiter, weights, bed, diffusivity):
    cond_here = flow.shape[0]
    wet_mask = wet.astype(jnp.float32)[:, None]
    limit_mask = limiter.astype(jnp.float32)
    state_now = flow
    bed_change = jnp.zeros((cond_here,) + flow.shape[2:], jnp.float32)
    for stepper in range(STEPS):
        rim_rows = flow_rim(state_now, depth)
        state_now = second_section(state_now, rim_rows, depth, wet_mask, forcing)
        flux_first, flux_second = transport(state_now, limit_mask)
        flux_rows = with_halo(flux_first, (("space", 1),), 1)
        bed_change = bed_change - morph_factor * (rows_diff(flux_rows) + column_diff(flux_second))
    weight_all = weights.astype(jnp.float32)
    weight_mine = lax.dynamic_slice_in_dim(
        weight_all, lax.axis_index("cond") * cond_here, cond_here
    )
    own_part = jnp.sum(weight_mine[:, None, None] * bed_change, 0) / jnp.sum(weight_all)
    portion = lax.psum(own_part, "cond")
    padded = rim_cells(diffusivity)
    centre = padded[1:-1, 1:-1]
    coefs = [centre * other / (centre + other) for other in neighbours(padded)]
    rhs = bed + portion
    solution = jnp.zeros_like(rhs)
    image = apply_op(rhs, coefs)
    totals = reduce_all(jnp.stack([jnp.sum(rhs * rhs), jnp.sum(rhs * image)]))
    norm_now = totals[0]
    alpha = norm_now / totals[1]
    residual, direction, along = (rhs, rhs, image)
    for sweep in range(ITERS):
        solution = solution + alpha * direction
        if sweep + 1 < ITERS:
            residual = residual - alpha * along
            image = apply_op(residual, coefs)
            totals = reduce_all(
                jnp.stack([jnp.sum(residual * residual), jnp.sum(residual * image)])
            )
            ratio = totals[0] / norm_now
            alpha = totals[0] / (totals[1] - ratio * totals[0] / alpha)
            direction = residual + ratio * direction
            along = image + ratio * along
            norm_now = totals[0]
    return (state_now[:, 0], solution)


def solution(mesh):
    in_specs = (
        P("cond", None, "space", None),
        P("cond", None, "space", None),
        P("cond", "space", None),
        P("space", None),
        P("space", None),
        P(),
        P("space", None),
        P("space", None),
    )
    out_specs = (P("cond", "space", None), P("space", None))
    return jax.shard_map(local, mesh=mesh, in_specs=in_specs, out_specs=out_specs, check_vma=False)
```

profile of v0, /device:TPU:0, one launch (start us, length us, event | category | flops | bytes accessed | tf_op | source)
XLA Modules:
  0.0 204.6 jit_solution(7893001801209511206)
XLA Ops:
  8.4 2.5 %collective-permute-start = (f32[2,2,1,2048]{3,2,0,1:T(1,128)S(1)}, f32[2,2,1,2048]{3,2,0,1:T(1,128)S(1)}, u32[]{:S(2)}, u32[]{:S(2)}) collective-permute-start(f32[2,2,1,2048]{3,2,0,1:T(1,128)S(1)} %get-tuple-element.99), channel_id=1, source_target_pairs={{0,1},{1,2},{2,3},{3,4},{4,5},{5,6},{6,7},{8,9},{9,10},{10,11},{11... | collective-permute-start | bytes 98312 | tf_op jit(solution)/shard_map/ppermute | solution.py:24
  11.0 1.3 collective-permute-start.1
  12.3 3.9 %collective-permute-done.1 = f32[2,2,1,2048]{3,2,0,1:T(1,128)S(1)} collective-permute-done((f32[2,2,1,2048]{3,2,0,1:T(1,128)S(1)}, f32[2,2,1,2048]{3,2,0,1:T(1,128)S(1)}, u32[]{:S(2)}, u32[]{:S(2)}) %collective-permute-start.1) | collective-permute-done | bytes 32800 | tf_op jit(solution)/shard_map/ppermute | solution.py:26
  18.3 4.5 %collective-permute-start.2 = (f32[2,2,1,2048]{3,2,0,1:T(1,128)S(1)}, f32[2,2,1,2048]{3,2,0,1:T(1,128)S(1)}, u32[]{:S(2)}, u32[]{:S(2)}) collective-permute-start(f32[2,2,1,2048]{3,2,0,1:T(1,128)S(1)} %get-tuple-element.97), channel_id=1, source_target_pairs={{0,1},{1,2},{2,3},{3,4},{4,5},{5,6},{6,7},{8,9},{9,10},{10,11},{11... | collective-permute-start | bytes 98312 | tf_op jit(solution)/shard_map/ppermute | solution.py:24
  22.9 1.3 collective-permute-start.3
  24.2 1.8 collective-permute-done.3
  27.0 4.1 %collective-permute-start.4 = (f32[2,2,1,2048]{3,2,0,1:T(1,128)S(1)}, f32[2,2,1,2048]{3,2,0,1:T(1,128)S(1)}, u32[]{:S(2)}, u32[]{:S(2)}) collective-permute-start(f32[2,2,1,2048]{3,2,0,1:T(1,128)S(1)} %get-tuple-element.95), channel_id=1, source_target_pairs={{0,1},{1,2},{2,3},{3,4},{4,5},{5,6},{6,7},{8,9},{9,10},{10,11},{11... | collective-permute-start | bytes 98312 | tf_op jit(solution)/shard_map/ppermute | solution.py:24
  32.4 1.8 collective-permute-done.5
  35.2 4.1 %collective-permute-start.6 = (f32[2,2,1,2048]{3,2,0,1:T(1,128)S(1)}, f32[2,2,1,2048]{3,2,0,1:T(1,128)S(1)}, u32[]{:S(2)}, u32[]{:S(2)}) collective-permute-start(f32[2,2,1,2048]{3,2,0,1:T(1,128)S(1)} %get-tuple-element.93), channel_id=1, source_target_pairs={{0,1},{1,2},{2,3},{3,4},{4,5},{5,6},{6,7},{8,9},{9,10},{10,11},{11... | collective-permute-start | bytes 98312 | tf_op jit(solution)/shard_map/ppermute | solution.py:24
  40.6 1.8 collective-permute-done.7
  43.6 4.1 %collective-permute-start.8 = (f32[2,2,1,2048]{3,2,0,1:T(1,128)S(1)}, f32[2,2,1,2048]{3,2,0,1:T(1,128)S(1)}, u32[]{:S(2)}, u32[]{:S(2)}) collective-permute-start(f32[2,2,1,2048]{3,2,0,1:T(1,128)S(1)} %get-tuple-element.91), channel_id=1, source_target_pairs={{0,1},{1,2},{2,3},{3,4},{4,5},{5,6},{6,7},{8,9},{9,10},{10,11},{11... | collective-permute-start | bytes 98312 | tf_op jit(solution)/shard_map/ppermute | solution.py:24
  48.9 1.8 collective-permute-done.9
  52.1 4.1 %collective-permute-start.10 = (f32[2,2,1,2048]{3,2,0,1:T(1,128)S(1)}, f32[2,2,1,2048]{3,2,0,1:T(1,128)S(1)}, u32[]{:S(2)}, u32[]{:S(2)}) collective-permute-start(f32[2,2,1,2048]{3,2,0,1:T(1,128)S(1)} %get-tuple-element.89), channel_id=1, source_target_pairs={{0,1},{1,2},{2,3},{3,4},{4,5},{5,6},{6,7},{8,9},{9,10},{10,11},{11... | collective-permute-start | bytes 98312 | tf_op jit(solution)/shard_map/ppermute | solution.py:24
  57.5 1.3 collective-permute-start.16
  58.8 3.7 %collective-permute-start.17 = (f32[2,1,2048]{2,1,0:T(1,128)S(1)}, f32[2,1,2048]{2,1,0:T(1,128)S(1)}, u32[]{:S(2)}, u32[]{:S(2)}) collective-permute-start(f32[2,1,2048]{2,1,0:T(1,128)S(1)} %get-tuple-element.102), channel_id=1, source_target_pairs={{0,1},{1,2},{2,3},{3,4},{4,5},{5,6},{6,7},{8,9},{9,10},{10,11},{11... | collective-permute-start | bytes 49160 | tf_op jit(solution)/shard_map/ppermute | solution.py:24
  63.9 3.6 %collective-permute-start.12 = (f32[2,2,1,2048]{3,2,0,1:T(1,128)S(1)}, f32[2,2,1,2048]{3,2,0,1:T(1,128)S(1)}, u32[]{:S(2)}, u32[]{:S(2)}) collective-permute-start(f32[2,2,1,2048]{3,2,0,1:T(1,128)S(1)} %get-tuple-element.87), channel_id=1, source_target_pairs={{0,1},{1,2},{2,3},{3,4},{4,5},{5,6},{6,7},{8,9},{9,10},{10,11},{11... | collective-permute-start | bytes 98312 | tf_op jit(solution)/shard_map/ppermute | solution.py:24
  67.5 1.3 collective-permute-start.13
  68.9 1.3 collective-permute-start.18
  72.1 4.1 %collective-permute-start.14 = (f32[2,2,1,2048]{3,2,0,1:T(1,128)S(1)}, f32[2,2,1,2048]{3,2,0,1:T(1,128)S(1)}, u32[]{:S(2)}, u32[]{:S(2)}) collective-permute-start(f32[2,2,1,2048]{3,2,0,1:T(1,128)S(1)} %get-tuple-element.85), channel_id=1, source_target_pairs={{0,1},{1,2},{2,3},{3,4},{4,5},{5,6},{6,7},{8,9},{9,10},{10,11},{11... | collective-permute-start | bytes 98312 | tf_op jit(solution)/shard_map/ppermute | solution.py:24
  77.5 3.4 %collective-permute-start.19 = (f32[2,1,2048]{2,1,0:T(1,128)S(1)}, f32[2,1,2048]{2,1,0:T(1,128)S(1)}, u32[]{:S(2)}, u32[]{:S(2)}) collective-permute-start(f32[2,1,2048]{2,1,0:T(1,128)S(1)} %get-tuple-element.104), channel_id=1, source_target_pairs={{0,1},{1,2},{2,3},{3,4},{4,5},{5,6},{6,7},{8,9},{9,10},{10,11},{11... | collective-permute-start | bytes 49160 | tf_op jit(solution)/shard_map/ppermute | solution.py:24
  84.0 4.3 %collective-permute-start.21 = (f32[2,1,2048]{2,1,0:T(1,128)S(1)}, f32[2,1,2048]{2,1,0:T(1,128)S(1)}, u32[]{:S(2)}, u32[]{:S(2)}) collective-permute-start(f32[2,1,2048]{2,1,0:T(1,128)S(1)} %get-tuple-element.106), channel_id=1, source_target_pairs={{0,1},{1,2},{2,3},{3,4},{4,5},{5,6},{6,7},{8,9},{9,10},{10,11},{11... | collective-permute-start | bytes 49160 | tf_op jit(solution)/shard_map/ppermute | solution.py:24
  89.6 4.5 %collective-permute-start.23 = (f32[2,1,2048]{2,1,0:T(1,128)S(1)}, f32[2,1,2048]{2,1,0:T(1,128)S(1)}, u32[]{:S(2)}, u32[]{:S(2)}) collective-permute-start(f32[2,1,2048]{2,1,0:T(1,128)S(1)} %get-tuple-element.108), channel_id=1, source_target_pairs={{0,1},{1,2},{2,3},{3,4},{4,5},{5,6},{6,7},{8,9},{9,10},{10,11},{11... | collective-permute-start | bytes 49160 | tf_op jit(solution)/shard_map/ppermute | solution.py:24
  95.4 1.4 broadcast_divide_fusion
  97.7 3.6 %collective-permute-start.24 = (f32[1,2048]{1,0:T(1,128)S(1)}, f32[1,2048]{1,0:T(1,128)S(1)}, u32[]{:S(2)}, u32[]{:S(2)}) collective-permute-start(f32[1,2048]{1,0:T(1,128)S(1)} %get-tuple-element.111), channel_id=1, source_target_pairs={{0,1},{1,2},{2,3},{3,4},{4,5},{5,6},{6,7},{8,9},{9,10},{10,11},{11... | collective-permute-start | bytes 24584 | tf_op jit(solution)/shard_map/ppermute | solution.py:24
  102.6 40.1 %all-reduce.25.cloned.1.call-done = f32[16,2048]{1,0:T(8,128)} async-done(((f32[16,2048]{1,0:T(8,128)}), f32[16,2048]{1,0:T(8,128)}) %all-reduce.25.cloned.1.call-update) | async-done | bytes 131088 | tf_op jit(solution)/shard_map/psum | solution.py:113
  143.7 1.3 collective-permute-start.25
  146.5 3.3 %collective-permute-done.27 = f32[1,2048]{1,0:T(1,128)S(1)} collective-permute-done((f32[1,2048]{1,0:T(1,128)S(1)}, f32[1,2048]{1,0:T(1,128)S(1)}, u32[]{:S(2)}, u32[]{:S(2)}) %collective-permute-start.27) | collective-permute-done | bytes 8224 | tf_op jit(solution)/shard_map/ppermute | solution.py:26
  150.8 1.4 pad_maximum_fusion.38
  152.1 16.0 %psum.22 = f32[2]{0:T(128)S(1)} all-reduce(f32[2]{0:T(128)S(1)} %pad_maximum_fusion.38), channel_id=1, replica_groups=mesh['cond'=4,'space'=8] {'space'}, use_global_device_ids=true, to_apply=%region_5.6 | all-reduce | flops 2 | bytes 16 | tf_op jit(solution)/shard_map/psum | solution.py:82
  172.7 1.8 collective-permute-done.29
  175.5 1.4 pad_maximum_fusion.39
  177.6 14.5 %psum.23 = f32[2]{0:T(128)S(1)} all-reduce(f32[2]{0:T(128)S(1)} %pad_maximum_fusion.39), channel_id=1, replica_groups=mesh['cond'=4,'space'=8] {'space'}, use_global_device_ids=true, to_apply=%region_8.9 | all-reduce | flops 2 | bytes 16 | tf_op jit(solution)/shard_map/psum | solution.py:82
  (133 shorter events, 35.1 us)
Async XLA Ops:
  7.2 135.5 %all-reduce.25.cloned.1.call-start = ((), (), s32[]{:S(2)}) async-start(), calls=%async_computation | async-start | bytes 262144 | tf_op jit(solution)/shard_map/psum | solution.py:113
  8.4 3.9 %collective-permute-start = (f32[2,2,1,2048]{3,2,0,1:T(1,128)S(1)}, f32[2,2,1,2048]{3,2,0,1:T(1,128)S(1)}, u32[]{:S(2)}, u32[]{:S(2)}) collective-permute-start(f32[2,2,1,2048]{3,2,0,1:T(1,128)S(1)} %get-tuple-element.99), channel_id=1, source_target_pairs={{0,1},{1,2},{2,3},{3,4},{4,5},{5,6},{6,7},{8,9},{9,10},{10,11},{11... | collective-permute-start | bytes 98312 | tf_op jit(solution)/shard_map/ppermute | solution.py:24
  11.0 5.3 %collective-permute-start.1 = (f32[2,2,1,2048]{3,2,0,1:T(1,128)S(1)}, f32[2,2,1,2048]{3,2,0,1:T(1,128)S(1)}, u32[]{:S(2)}, u32[]{:S(2)}) collective-permute-start(f32[2,2,1,2048]{3,2,0,1:T(1,128)S(1)} %get-tuple-element.100), channel_id=1, source_target_pairs={{1,0},{2,1},{3,2},{4,3},{5,4},{6,5},{7,6},{9,8},{10,9},{11,10},{12... | collective-permute-start | bytes 98312 | tf_op jit(solution)/shard_map/ppermute | solution.py:26
  18.3 5.8 %collective-permute-start.2 = (f32[2,2,1,2048]{3,2,0,1:T(1,128)S(1)}, f32[2,2,1,2048]{3,2,0,1:T(1,128)S(1)}, u32[]{:S(2)}, u32[]{:S(2)}) collective-permute-start(f32[2,2,1,2048]{3,2,0,1:T(1,128)S(1)} %get-tuple-element.97), channel_id=1, source_target_pairs={{0,1},{1,2},{2,3},{3,4},{4,5},{5,6},{6,7},{8,9},{9,10},{10,11},{11... | collective-permute-start | bytes 98312 | tf_op jit(solution)/shard_map/ppermute | solution.py:24
  22.9 3.1 %collective-permute-start.3 = (f32[2,2,1,2048]{3,2,0,1:T(1,128)S(1)}, f32[2,2,1,2048]{3,2,0,1:T(1,128)S(1)}, u32[]{:S(2)}, u32[]{:S(2)}) collective-permute-start(f32[2,2,1,2048]{3,2,0,1:T(1,128)S(1)} %get-tuple-element.98), channel_id=1, source_target_pairs={{1,0},{2,1},{3,2},{4,3},{5,4},{6,5},{7,6},{9,8},{10,9},{11,10},{12... | collective-permute-start | bytes 98312 | tf_op jit(solution)/shard_map/ppermute | solution.py:26
  27.0 5.4 %collective-permute-start.4 = (f32[2,2,1,2048]{3,2,0,1:T(1,128)S(1)}, f32[2,2,1,2048]{3,2,0,1:T(1,128)S(1)}, u32[]{:S(2)}, u32[]{:S(2)}) collective-permute-start(f32[2,2,1,2048]{3,2,0,1:T(1,128)S(1)} %get-tuple-element.95), channel_id=1, source_target_pairs={{0,1},{1,2},{2,3},{3,4},{4,5},{5,6},{6,7},{8,9},{9,10},{10,11},{11... | collective-permute-start | bytes 98312 | tf_op jit(solution)/shard_map/ppermute | solution.py:24
  31.0 3.1 %collective-permute-start.5 = (f32[2,2,1,2048]{3,2,0,1:T(1,128)S(1)}, f32[2,2,1,2048]{3,2,0,1:T(1,128)S(1)}, u32[]{:S(2)}, u32[]{:S(2)}) collective-permute-start(f32[2,2,1,2048]{3,2,0,1:T(1,128)S(1)} %get-tuple-element.96), channel_id=1, source_target_pairs={{1,0},{2,1},{3,2},{4,3},{5,4},{6,5},{7,6},{9,8},{10,9},{11,10},{12... | collective-permute-start | bytes 98312 | tf_op jit(solution)/shard_map/ppermute | solution.py:26
  35.2 5.4 %collective-permute-start.6 = (f32[2,2,1,2048]{3,2,0,1:T(1,128)S(1)}, f32[2,2,1,2048]{3,2,0,1:T(1,128)S(1)}, u32[]{:S(2)}, u32[]{:S(2)}) collective-permute-start(f32[2,2,1,2048]{3,2,0,1:T(1,128)S(1)} %get-tuple-element.93), channel_id=1, source_target_pairs={{0,1},{1,2},{2,3},{3,4},{4,5},{5,6},{6,7},{8,9},{9,10},{10,11},{11... | collective-permute-start | bytes 98312 | tf_op jit(solution)/shard_map/ppermute | solution.py:24
  39.3 3.1 %collective-permute-start.7 = (f32[2,2,1,2048]{3,2,0,1:T(1,128)S(1)}, f32[2,2,1,2048]{3,2,0,1:T(1,128)S(1)}, u32[]{:S(2)}, u32[]{:S(2)}) collective-permute-start(f32[2,2,1,2048]{3,2,0,1:T(1,128)S(1)} %get-tuple-element.94), channel_id=1, source_target_pairs={{1,0},{2,1},{3,2},{4,3},{5,4},{6,5},{7,6},{9,8},{10,9},{11,10},{12... | collective-permute-start | bytes 98312 | tf_op jit(solution)/shard_map/ppermute | solution.py:26
  43.6 5.4 %collective-permute-start.8 = (f32[2,2,1,2048]{3,2,0,1:T(1,128)S(1)}, f32[2,2,1,2048]{3,2,0,1:T(1,128)S(1)}, u32[]{:S(2)}, u32[]{:S(2)}) collective-permute-start(f32[2,2,1,2048]{3,2,0,1:T(1,128)S(1)} %get-tuple-element.91), channel_id=1, source_target_pairs={{0,1},{1,2},{2,3},{3,4},{4,5},{5,6},{6,7},{8,9},{9,10},{10,11},{11... | collective-permute-start | bytes 98312 | tf_op jit(solution)/shard_map/ppermute | solution.py:24
  47.6 3.1 %collective-permute-start.9 = (f32[2,2,1,2048]{3,2,0,1:T(1,128)S(1)}, f32[2,2,1,2048]{3,2,0,1:T(1,128)S(1)}, u32[]{:S(2)}, u32[]{:S(2)}) collective-permute-start(f32[2,2,1,2048]{3,2,0,1:T(1,128)S(1)} %get-tuple-element.92), channel_id=1, source_target_pairs={{1,0},{2,1},{3,2},{4,3},{5,4},{6,5},{7,6},{9,8},{10,9},{11,10},{12... | collective-permute-start | bytes 98312 | tf_op jit(solution)/shard_map/ppermute | solution.py:26
  52.1 10.4 %collective-permute-start.10 = (f32[2,2,1,2048]{3,2,0,1:T(1,128)S(1)}, f32[2,2,1,2048]{3,2,0,1:T(1,128)S(1)}, u32[]{:S(2)}, u32[]{:S(2)}) collective-permute-start(f32[2,2,1,2048]{3,2,0,1:T(1,128)S(1)} %get-tuple-element.89), channel_id=1, source_target_pairs={{0,1},{1,2},{2,3},{3,4},{4,5},{5,6},{6,7},{8,9},{9,10},{10,11},{11... | collective-permute-start | bytes 98312 | tf_op jit(solution)/shard_map/ppermute | solution.py:24
  56.1 6.3 %collective-permute-start.11 = (f32[2,2,1,2048]{3,2,0,1:T(1,128)S(1)}, f32[2,2,1,2048]{3,2,0,1:T(1,128)S(1)}, u32[]{:S(2)}, u32[]{:S(2)}) collective-permute-start(f32[2,2,1,2048]{3,2,0,1:T(1,128)S(1)} %get-tuple-element.90), channel_id=1, source_target_pairs={{1,0},{2,1},{3,2},{4,3},{5,4},{6,5},{7,6},{9,8},{10,9},{11,10},{12... | collective-permute-start | bytes 98312 | tf_op jit(solution)/shard_map/ppermute | solution.py:26
  57.5 26.5 %collective-permute-start.16 = (f32[2,1,2048]{2,1,0:T(1,128)S(1)}, f32[2,1,2048]{2,1,0:T(1,128)S(1)}, u32[]{:S(2)}, u32[]{:S(2)}) collective-permute-start(f32[2,1,2048]{2,1,0:T(1,128)S(1)} %get-tuple-element.101), channel_id=1, source_target_pairs={{1,0},{2,1},{3,2},{4,3},{5,4},{6,5},{7,6},{9,8},{10,9},{11,10},{12... | collective-permute-start | bytes 49160 | tf_op jit(solution)/shard_map/ppermute | solution.py:26
  58.8 29.5 %collective-permute-start.17 = (f32[2,1,2048]{2,1,0:T(1,128)S(1)}, f32[2,1,2048]{2,1,0:T(1,128)S(1)}, u32[]{:S(2)}, u32[]{:S(2)}) collective-permute-start(f32[2,1,2048]{2,1,0:T(1,128)S(1)} %get-tuple-element.102), channel_id=1, source_target_pairs={{0,1},{1,2},{2,3},{3,4},{4,5},{5,6},{6,7},{8,9},{9,10},{10,11},{11... | collective-permute-start | bytes 49160 | tf_op jit(solution)/shard_map/ppermute | solution.py:24
  63.9 6.3 %collective-permute-start.12 = (f32[2,2,1,2048]{3,2,0,1:T(1,128)S(1)}, f32[2,2,1,2048]{3,2,0,1:T(1,128)S(1)}, u32[]{:S(2)}, u32[]{:S(2)}) collective-permute-start(f32[2,2,1,2048]{3,2,0,1:T(1,128)S(1)} %get-tuple-element.87), channel_id=1, source_target_pairs={{0,1},{1,2},{2,3},{3,4},{4,5},{5,6},{6,7},{8,9},{9,10},{10,11},{11... | collective-permute-start | bytes 98312 | tf_op jit(solution)/shard_map/ppermute | solution.py:24
  67.5 3.1 %collective-permute-start.13 = (f32[2,2,1,2048]{3,2,0,1:T(1,128)S(1)}, f32[2,2,1,2048]{3,2,0,1:T(1,128)S(1)}, u32[]{:S(2)}, u32[]{:S(2)}) collective-permute-start(f32[2,2,1,2048]{3,2,0,1:T(1,128)S(1)} %get-tuple-element.88), channel_id=1, source_target_pairs={{1,0},{2,1},{3,2},{4,3},{5,4},{6,5},{7,6},{9,8},{10,9},{11,10},{12... | collective-permute-start | bytes 98312 | tf_op jit(solution)/shard_map/ppermute | solution.py:26
  68.9 20.7 %collective-permute-start.18 = (f32[2,1,2048]{2,1,0:T(1,128)S(1)}, f32[2,1,2048]{2,1,0:T(1,128)S(1)}, u32[]{:S(2)}, u32[]{:S(2)}) collective-permute-start(f32[2,1,2048]{2,1,0:T(1,128)S(1)} %get-tuple-element.103), channel_id=1, source_target_pairs={{1,0},{2,1},{3,2},{4,3},{5,4},{6,5},{7,6},{9,8},{10,9},{11,10},{12... | collective-permute-start | bytes 49160 | tf_op jit(solution)/shard_map/ppermute | solution.py:26
  72.1 5.4 %collective-permute-start.14 = (f32[2,2,1,2048]{3,2,0,1:T(1,128)S(1)}, f32[2,2,1,2048]{3,2,0,1:T(1,128)S(1)}, u32[]{:S(2)}, u32[]{:S(2)}) collective-permute-start(f32[2,2,1,2048]{3,2,0,1:T(1,128)S(1)} %get-tuple-element.85), channel_id=1, source_target_pairs={{0,1},{1,2},{2,3},{3,4},{4,5},{5,6},{6,7},{8,9},{9,10},{10,11},{11... | collective-permute-start | bytes 98312 | tf_op jit(solution)/shard_map/ppermute | solution.py:24
  76.2 4.8 %collective-permute-start.15 = (f32[2,2,1,2048]{3,2,0,1:T(1,128)S(1)}, f32[2,2,1,2048]{3,2,0,1:T(1,128)S(1)}, u32[]{:S(2)}, u32[]{:S(2)}) collective-permute-start(f32[2,2,1,2048]{3,2,0,1:T(1,128)S(1)} %get-tuple-element.86), channel_id=1, source_target_pairs={{1,0},{2,1},{3,2},{4,3},{5,4},{6,5},{7,6},{9,8},{10,9},{11,10},{12... | collective-permute-start | bytes 98312 | tf_op jit(solution)/shard_map/ppermute | solution.py:26
  77.5 17.2 %collective-permute-start.19 = (f32[2,1,2048]{2,1,0:T(1,128)S(1)}, f32[2,1,2048]{2,1,0:T(1,128)S(1)}, u32[]{:S(2)}, u32[]{:S(2)}) collective-permute-start(f32[2,1,2048]{2,1,0:T(1,128)S(1)} %get-tuple-element.104), channel_id=1, source_target_pairs={{0,1},{1,2},{2,3},{3,4},{4,5},{5,6},{6,7},{8,9},{9,10},{10,11},{11... | collective-permute-start | bytes 49160 | tf_op jit(solution)/shard_map/ppermute | solution.py:24
  81.0 13.8 %collective-permute-start.20 = (f32[2,1,2048]{2,1,0:T(1,128)S(1)}, f32[2,1,2048]{2,1,0:T(1,128)S(1)}, u32[]{:S(2)}, u32[]{:S(2)}) collective-permute-start(f32[2,1,2048]{2,1,0:T(1,128)S(1)} %get-tuple-element.105), channel_id=1, source_target_pairs={{1,0},{2,1},{3,2},{4,3},{5,4},{6,5},{7,6},{9,8},{10,9},{11,10},{12... | collective-permute-start | bytes 49160 | tf_op jit(solution)/shard_map/ppermute | solution.py:26
  84.0 10.8 %collective-permute-start.21 = (f32[2,1,2048]{2,1,0:T(1,128)S(1)}, f32[2,1,2048]{2,1,0:T(1,128)S(1)}, u32[]{:S(2)}, u32[]{:S(2)}) collective-permute-start(f32[2,1,2048]{2,1,0:T(1,128)S(1)} %get-tuple-element.106), channel_id=1, source_target_pairs={{0,1},{1,2},{2,3},{3,4},{4,5},{5,6},{6,7},{8,9},{9,10},{10,11},{11... | collective-permute-start | bytes 49160 | tf_op jit(solution)/shard_map/ppermute | solution.py:24
  88.3 6.5 %collective-permute-start.22 = (f32[2,1,2048]{2,1,0:T(1,128)S(1)}, f32[2,1,2048]{2,1,0:T(1,128)S(1)}, u32[]{:S(2)}, u32[]{:S(2)}) collective-permute-start(f32[2,1,2048]{2,1,0:T(1,128)S(1)} %get-tuple-element.107), channel_id=1, source_target_pairs={{1,0},{2,1},{3,2},{4,3},{5,4},{6,5},{7,6},{9,8},{10,9},{11,10},{12... | collective-permute-start | bytes 49160 | tf_op jit(solution)/shard_map/ppermute | solution.py:26
  89.6 5.2 %collective-permute-start.23 = (f32[2,1,2048]{2,1,0:T(1,128)S(1)}, f32[2,1,2048]{2,1,0:T(1,128)S(1)}, u32[]{:S(2)}, u32[]{:S(2)}) collective-permute-start(f32[2,1,2048]{2,1,0:T(1,128)S(1)} %get-tuple-element.108), channel_id=1, source_target_pairs={{0,1},{1,2},{2,3},{3,4},{4,5},{5,6},{6,7},{8,9},{9,10},{10,11},{11... | collective-permute-start | bytes 49160 | tf_op jit(solution)/shard_map/ppermute | solution.py:24
  95.4 47.3 %copy-start.5 = (f32[16,2048]{1,0:T(8,128)S(1)}, f32[16,2048]{1,0:T(8,128)}, u32[]{:S(2)}) copy-start(f32[16,2048]{1,0:T(8,128)} %param.14) | copy-start | bytes 393220
  97.7 48.6 %collective-permute-start.24 = (f32[1,2048]{1,0:T(1,128)S(1)}, f32[1,2048]{1,0:T(1,128)S(1)}, u32[]{:S(2)}, u32[]{:S(2)}) collective-permute-start(f32[1,2048]{1,0:T(1,128)S(1)} %get-tuple-element.111), channel_id=1, source_target_pairs={{0,1},{1,2},{2,3},{3,4},{4,5},{5,6},{6,7},{8,9},{9,10},{10,11},{11... | collective-permute-start | bytes 24584 | tf_op jit(solution)/shard_map/ppermute | solution.py:24
  101.3 44.9 %collective-permute-start.26 = (f32[1,2048]{1,0:T(1,128)S(1)}, f32[1,2048]{1,0:T(1,128)S(1)}, u32[]{:S(2)}, u32[]{:S(2)}) collective-permute-start(f32[1,2048]{1,0:T(1,128)S(1)} %get-tuple-element.112), channel_id=1, source_target_pairs={{1,0},{2,1},{3,2},{4,3},{5,4},{6,5},{7,6},{9,8},{10,9},{11,10},{12... | collective-permute-start | bytes 24584 | tf_op jit(solution)/shard_map/ppermute | solution.py:26
  143.7 2.8 %collective-permute-start.25 = (f32[1,2048]{1,0:T(1,128)S(1)}, f32[1,2048]{1,0:T(1,128)S(1)}, u32[]{:S(2)}, u32[]{:S(2)}) collective-permute-start(f32[1,2048]{1,0:T(1,128)S(1)} %get-tuple-element.113), channel_id=1, source_target_pairs={{0,1},{1,2},{2,3},{3,4},{4,5},{5,6},{6,7},{8,9},{9,10},{10,11},{11... | collective-permute-start | bytes 24584 | tf_op jit(solution)/shard_map/ppermute | solution.py:24
  145.0 4.8 %collective-permute-start.27 = (f32[1,2048]{1,0:T(1,128)S(1)}, f32[1,2048]{1,0:T(1,128)S(1)}, u32[]{:S(2)}, u32[]{:S(2)}) collective-permute-start(f32[1,2048]{1,0:T(1,128)S(1)} %get-tuple-element.114), channel_id=1, source_target_pairs={{1,0},{2,1},{3,2},{4,3},{5,4},{6,5},{7,6},{9,8},{10,9},{11,10},{12... | collective-permute-start | bytes 24584 | tf_op jit(solution)/shard_map/ppermute | solution.py:26
  170.1 2.6 %collective-permute-start.28 = (f32[1,2048]{1,0:T(1,128)S(1)}, f32[1,2048]{1,0:T(1,128)S(1)}, u32[]{:S(2)}, u32[]{:S(2)}) collective-permute-start(f32[1,2048]{1,0:T(1,128)S(1)} %get-tuple-element.109), channel_id=1, source_target_pairs={{0,1},{1,2},{2,3},{3,4},{4,5},{5,6},{6,7},{8,9},{9,10},{10,11},{11... | collective-permute-start | bytes 24584 | tf_op jit(solution)/shard_map/ppermute | solution.py:24
  171.4 3.1 %collective-permute-start.29 = (f32[1,2048]{1,0:T(1,128)S(1)}, f32[1,2048]{1,0:T(1,128)S(1)}, u32[]{:S(2)}, u32[]{:S(2)}) collective-permute-start(f32[1,2048]{1,0:T(1,128)S(1)} %get-tuple-element.110), channel_id=1, source_target_pairs={{1,0},{2,1},{3,2},{4,3},{5,4},{6,5},{7,6},{9,8},{10,9},{11,10},{12... | collective-permute-start | bytes 24584 | tf_op jit(solution)/shard_map/ppermute | solution.py:26
  (7 other events, 19.7 us)
Sparse Core Ops, SparseCore 0:
  96.9 45.7 all-reduce.24
where the time goes:
time: 206 us; the launch traced here: 205 us
  starting transfers between devices  72.4 us (35%)
  waiting for transfers between devices  56.7 us (28%)
  blocking collectives  30.5 us (15%)
  between operations  20.6 us (10%)
  other arithmetic  19.7 us (10%)
  local copies, waits for them, and re-layouts  4.73 us (2%)
    ppermute x15, starting transfers between devices, with_halo(): lax.ppermute(tail, axis, [(i, (i + 1) % count) for i in range(ends)])  53 us
    psum x1, waiting for transfers between devices, local(): portion = lax.psum(own_part, 'cond')  40.1 us
    psum x2, blocking collectives, reduce_all(): return lax.psum(values, 'space')  30.5 us
    ppermute x15, starting transfers between devices, with_halo(): lax.ppermute(head, axis, [((i + 1) % count, i) for i in range(ends)])  19.4 us
    ppermute x15, waiting for transfers between devices, with_halo(): lax.ppermute(head, axis, [((i + 1) % count, i) for i in range(ends)])  16.6 us
  transfers between devices with their start and end apart: 31, of which 9 were waited for; matrix products, arithmetic and copies ran while one was open for 3% of the time, Pallas kernels for 0%

commit v1 on v0

--- a/solution.py
+++ b/solution.py
@@ -110,7 +110,7 @@
         weight_all, lax.axis_index("cond") * cond_here, cond_here
     )
     own_part = jnp.sum(weight_mine[:, None, None] * bed_change, 0) / jnp.sum(weight_all)
-    portion = lax.psum(own_part, "cond")
+    portion = jnp.sum(lax.all_gather(own_part, "cond"), axis=0)
     padded = rim_cells(diffusivity)
     centre = padded[1:-1, 1:-1]
     coefs = [centre * other / (centre + other) for other in neighbours(padded)]

time: 206 us -> 162 us (0.79)
  waiting for transfers between devices: 56.7 us -> 16.3 us
  between operations: 20.6 us -> 7.37 us
  blocking collectives: 30.5 us -> 41.7 us
    psum x1 -> x0, waiting for transfers between devices: 40.1 us -> none  [local(): portion = lax.psum(own_part, 'cond')]
    all_gather x0 -> x1, blocking collectives: none -> 11.4 us  [local(): portion = jnp.sum(lax.all_gather(own_part, 'cond'), axis=0)]
  transfers between devices with their start and end apart: 31 -> 30, of which waited for: 9 -> 8; matrix products, arithmetic and copies ran while one was open for 3% -> 4% of each run, Pallas kernels for 0% -> 0%
where the time goes in v1:
time: 162 us; the launch traced here: 161 us
  starting transfers between devices  72.5 us (45%)
  blocking collectives  41.7 us (26%)
  other arithmetic  18.1 us (11%)
  waiting for transfers between devices  16.3 us (10%)
  between operations  7.37 us (5%)
  local copies, waits for them, and re-layouts  4.72 us (3%)
    ppermute x15, starting transfers between devices, with_halo(): lax.ppermute(tail, axis, [(i, (i + 1) % count) for i in range(ends)])  53 us
    psum x2, blocking collectives, reduce_all(): return lax.psum(values, 'space')  30.2 us
    ppermute x15, starting transfers between devices, with_halo(): lax.ppermute(head, axis, [((i + 1) % count, i) for i in range(ends)])  19.6 us
    ppermute x15, waiting for transfers between devices, with_halo(): lax.ppermute(head, axis, [((i + 1) % count, i) for i in range(ends)])  16.3 us
    all_gather x1, blocking collectives, local(): portion = jnp.sum(lax.all_gather(own_part, 'cond'), axis=0)  11.4 us
  transfers between devices with their start and end apart: 30, of which 8 were waited for; matrix products, arithmetic and copies ran while one was open for 4% of the time, Pallas kernels for 0%

profile of v1, /device:TPU:0, one launch (start us, length us, event | category | flops | bytes accessed | tf_op | source)
XLA Modules:
  0.0 160.7 jit_solution(3917779197810320199)
XLA Ops:
  1.9 2.5 %collective-permute-start = (f32[2,2,1,2048]{3,2,0,1:T(1,128)S(1)}, f32[2,2,1,2048]{3,2,0,1:T(1,128)S(1)}, u32[]{:S(2)}, u32[]{:S(2)}) collective-permute-start(f32[2,2,1,2048]{3,2,0,1:T(1,128)S(1)} %get-tuple-element.99), channel_id=1, source_target_pairs={{0,1},{1,2},{2,3},{3,4},{4,5},{5,6},{6,7},{8,9},{9,10},{10,11},{11... | collective-permute-start | bytes 98312 | tf_op jit(solution)/shard_map/ppermute | solution.py:24
  4.4 1.3 collective-permute-start.1
  5.7 3.9 %collective-permute-done.1 = f32[2,2,1,2048]{3,2,0,1:T(1,128)S(1)} collective-permute-done((f32[2,2,1,2048]{3,2,0,1:T(1,128)S(1)}, f32[2,2,1,2048]{3,2,0,1:T(1,128)S(1)}, u32[]{:S(2)}, u32[]{:S(2)}) %collective-permute-start.1) | collective-permute-done | bytes 32800 | tf_op jit(solution)/shard_map/ppermute | solution.py:26
  11.8 4.5 %collective-permute-start.2 = (f32[2,2,1,2048]{3,2,0,1:T(1,128)S(1)}, f32[2,2,1,2048]{3,2,0,1:T(1,128)S(1)}, u32[]{:S(2)}, u32[]{:S(2)}) collective-permute-start(f32[2,2,1,2048]{3,2,0,1:T(1,128)S(1)} %get-tuple-element.97), channel_id=1, source_target_pairs={{0,1},{1,2},{2,3},{3,4},{4,5},{5,6},{6,7},{8,9},{9,10},{10,11},{11... | collective-permute-start | bytes 98312 | tf_op jit(solution)/shard_map/ppermute | solution.py:24
  16.3 1.3 collective-permute-start.3
  17.6 1.8 %collective-permute-done.3 = f32[2,2,1,2048]{3,2,0,1:T(1,128)S(1)} collective-permute-done((f32[2,2,1,2048]{3,2,0,1:T(1,128)S(1)}, f32[2,2,1,2048]{3,2,0,1:T(1,128)S(1)}, u32[]{:S(2)}, u32[]{:S(2)}) %collective-permute-start.3) | collective-permute-done | bytes 32800 | tf_op jit(solution)/shard_map/ppermute | solution.py:26
  20.4 4.1 %collective-permute-start.4 = (f32[2,2,1,2048]{3,2,0,1:T(1,128)S(1)}, f32[2,2,1,2048]{3,2,0,1:T(1,128)S(1)}, u32[]{:S(2)}, u32[]{:S(2)}) collective-permute-start(f32[2,2,1,2048]{3,2,0,1:T(1,128)S(1)} %get-tuple-element.95), channel_id=1, source_target_pairs={{0,1},{1,2},{2,3},{3,4},{4,5},{5,6},{6,7},{8,9},{9,10},{10,11},{11... | collective-permute-start | bytes 98312 | tf_op jit(solution)/shard_map/ppermute | solution.py:24
  25.8 1.8 %collective-permute-done.5 = f32[2,2,1,2048]{3,2,0,1:T(1,128)S(1)} collective-permute-done((f32[2,2,1,2048]{3,2,0,1:T(1,128)S(1)}, f32[2,2,1,2048]{3,2,0,1:T(1,128)S(1)}, u32[]{:S(2)}, u32[]{:S(2)}) %collective-permute-start.5) | collective-permute-done | bytes 32800 | tf_op jit(solution)/shard_map/ppermute | solution.py:26
  28.6 4.1 %collective-permute-start.6 = (f32[2,2,1,2048]{3,2,0,1:T(1,128)S(1)}, f32[2,2,1,2048]{3,2,0,1:T(1,128)S(1)}, u32[]{:S(2)}, u32[]{:S(2)}) collective-permute-start(f32[2,2,1,2048]{3,2,0,1:T(1,128)S(1)} %get-tuple-element.93), channel_id=1, source_target_pairs={{0,1},{1,2},{2,3},{3,4},{4,5},{5,6},{6,7},{8,9},{9,10},{10,11},{11... | collective-permute-start | bytes 98312 | tf_op jit(solution)/shard_map/ppermute | solution.py:24
  34.0 1.8 %collective-permute-done.7 = f32[2,2,1,2048]{3,2,0,1:T(1,128)S(1)} collective-permute-done((f32[2,2,1,2048]{3,2,0,1:T(1,128)S(1)}, f32[2,2,1,2048]{3,2,0,1:T(1,128)S(1)}, u32[]{:S(2)}, u32[]{:S(2)}) %collective-permute-start.7) | collective-permute-done | bytes 32800 | tf_op jit(solution)/shard_map/ppermute | solution.py:26
  37.0 4.1 %collective-permute-start.8 = (f32[2,2,1,2048]{3,2,0,1:T(1,128)S(1)}, f32[2,2,1,2048]{3,2,0,1:T(1,128)S(1)}, u32[]{:S(2)}, u32[]{:S(2)}) collective-permute-start(f32[2,2,1,2048]{3,2,0,1:T(1,128)S(1)} %get-tuple-element.91), channel_id=1, source_target_pairs={{0,1},{1,2},{2,3},{3,4},{4,5},{5,6},{6,7},{8,9},{9,10},{10,11},{11... | collective-permute-start | bytes 98312 | tf_op jit(solution)/shard_map/ppermute | solution.py:24
  42.4 1.8 %collective-permute-done.9 = f32[2,2,1,2048]{3,2,0,1:T(1,128)S(1)} collective-permute-done((f32[2,2,1,2048]{3,2,0,1:T(1,128)S(1)}, f32[2,2,1,2048]{3,2,0,1:T(1,128)S(1)}, u32[]{:S(2)}, u32[]{:S(2)}) %collective-permute-start.9) | collective-permute-done | bytes 32800 | tf_op jit(solution)/shard_map/ppermute | solution.py:26
  45.5 4.1 %collective-permute-start.10 = (f32[2,2,1,2048]{3,2,0,1:T(1,128)S(1)}, f32[2,2,1,2048]{3,2,0,1:T(1,128)S(1)}, u32[]{:S(2)}, u32[]{:S(2)}) collective-permute-start(f32[2,2,1,2048]{3,2,0,1:T(1,128)S(1)} %get-tuple-element.89), channel_id=1, source_target_pairs={{0,1},{1,2},{2,3},{3,4},{4,5},{5,6},{6,7},{8,9},{9,10},{10,11},{11... | collective-permute-start | bytes 98312 | tf_op jit(solution)/shard_map/ppermute | solution.py:24
  52.2 3.7 %collective-permute-start.17 = (f32[2,1,2048]{2,1,0:T(1,128)S(1)}, f32[2,1,2048]{2,1,0:T(1,128)S(1)}, u32[]{:S(2)}, u32[]{:S(2)}) collective-permute-start(f32[2,1,2048]{2,1,0:T(1,128)S(1)} %get-tuple-element.102), channel_id=1, source_target_pairs={{0,1},{1,2},{2,3},{3,4},{4,5},{5,6},{6,7},{8,9},{9,10},{10,11},{11... | collective-permute-start | bytes 49160 | tf_op jit(solution)/shard_map/ppermute | solution.py:24
  57.3 3.6 %collective-permute-start.12 = (f32[2,2,1,2048]{3,2,0,1:T(1,128)S(1)}, f32[2,2,1,2048]{3,2,0,1:T(1,128)S(1)}, u32[]{:S(2)}, u32[]{:S(2)}) collective-permute-start(f32[2,2,1,2048]{3,2,0,1:T(1,128)S(1)} %get-tuple-element.87), channel_id=1, source_target_pairs={{0,1},{1,2},{2,3},{3,4},{4,5},{5,6},{6,7},{8,9},{9,10},{10,11},{11... | collective-permute-start | bytes 98312 | tf_op jit(solution)/shard_map/ppermute | solution.py:24
  65.6 4.1 %collective-permute-start.14 = (f32[2,2,1,2048]{3,2,0,1:T(1,128)S(1)}, f32[2,2,1,2048]{3,2,0,1:T(1,128)S(1)}, u32[]{:S(2)}, u32[]{:S(2)}) collective-permute-start(f32[2,2,1,2048]{3,2,0,1:T(1,128)S(1)} %get-tuple-element.85), channel_id=1, source_target_pairs={{0,1},{1,2},{2,3},{3,4},{4,5},{5,6},{6,7},{8,9},{9,10},{10,11},{11... | collective-permute-start | bytes 98312 | tf_op jit(solution)/shard_map/ppermute | solution.py:24
  71.0 3.4 %collective-permute-start.19 = (f32[2,1,2048]{2,1,0:T(1,128)S(1)}, f32[2,1,2048]{2,1,0:T(1,128)S(1)}, u32[]{:S(2)}, u32[]{:S(2)}) collective-permute-start(f32[2,1,2048]{2,1,0:T(1,128)S(1)} %get-tuple-element.104), channel_id=1, source_target_pairs={{0,1},{1,2},{2,3},{3,4},{4,5},{5,6},{6,7},{8,9},{9,10},{10,11},{11... | collective-permute-start | bytes 49160 | tf_op jit(solution)/shard_map/ppermute | solution.py:24
  74.4 1.3 collective-permute-start.20
  77.4 4.3 %collective-permute-start.21 = (f32[2,1,2048]{2,1,0:T(1,128)S(1)}, f32[2,1,2048]{2,1,0:T(1,128)S(1)}, u32[]{:S(2)}, u32[]{:S(2)}) collective-permute-start(f32[2,1,2048]{2,1,0:T(1,128)S(1)} %get-tuple-element.106), channel_id=1, source_target_pairs={{0,1},{1,2},{2,3},{3,4},{4,5},{5,6},{6,7},{8,9},{9,10},{10,11},{11... | collective-permute-start | bytes 49160 | tf_op jit(solution)/shard_map/ppermute | solution.py:24
  81.7 1.3 collective-permute-start.22
  83.0 4.3 %collective-permute-start.23 = (f32[2,1,2048]{2,1,0:T(1,128)S(1)}, f32[2,1,2048]{2,1,0:T(1,128)S(1)}, u32[]{:S(2)}, u32[]{:S(2)}) collective-permute-start(f32[2,1,2048]{2,1,0:T(1,128)S(1)} %get-tuple-element.108), channel_id=1, source_target_pairs={{0,1},{1,2},{2,3},{3,4},{4,5},{5,6},{6,7},{8,9},{9,10},{10,11},{11... | collective-permute-start | bytes 49160 | tf_op jit(solution)/shard_map/ppermute | solution.py:24
  88.0 3.6 %collective-permute-start.24 = (f32[1,2048]{1,0:T(1,128)S(1)}, f32[1,2048]{1,0:T(1,128)S(1)}, u32[]{:S(2)}, u32[]{:S(2)}) collective-permute-start(f32[1,2048]{1,0:T(1,128)S(1)} %get-tuple-element.111), channel_id=1, source_target_pairs={{0,1},{1,2},{2,3},{3,4},{4,5},{5,6},{6,7},{8,9},{9,10},{10,11},{11... | collective-permute-start | bytes 24584 | tf_op jit(solution)/shard_map/ppermute | solution.py:24
  91.7 1.5 collective-permute-start.26
  94.5 11.4 %all-gather = f32[64,2048]{1,0:T(8,128)S(1)} all-gather(f32[16,2048]{1,0:T(8,128)S(1)} %broadcast_divide_fusion), channel_id=2, replica_groups=mesh['cond'=4,'space'=8] {'cond'}, dimensions={0}, use_global_device_ids=true | all-gather | bytes 655360 | tf_op jit(solution)/shard_map/all_gather | solution.py:113
  106.8 1.4 collective-permute-start.25
  109.8 3.0 %collective-permute-done.27 = f32[1,2048]{1,0:T(1,128)S(1)} collective-permute-done((f32[1,2048]{1,0:T(1,128)S(1)}, f32[1,2048]{1,0:T(1,128)S(1)}, u32[]{:S(2)}, u32[]{:S(2)}) %collective-permute-start.27) | collective-permute-done | bytes 8224 | tf_op jit(solution)/shard_map/ppermute | solution.py:26
  113.8 1.4 pad_maximum_fusion.38
  115.2 16.0 %psum.14 = f32[2]{0:T(128)S(1)} all-reduce(f32[2]{0:T(128)S(1)} %pad_maximum_fusion.38), channel_id=1, replica_groups=mesh['cond'=4,'space'=8] {'space'}, use_global_device_ids=true, to_apply=%region_5.6 | all-reduce | flops 2 | bytes 16 | tf_op jit(solution)/shard_map/psum | solution.py:82
  134.4 1.3 collective-permute-start.29
  135.7 1.8 %collective-permute-done.29 = f32[1,2048]{1,0:T(1,128)S(1)} collective-permute-done((f32[1,2048]{1,0:T(1,128)S(1)}, f32[1,2048]{1,0:T(1,128)S(1)}, u32[]{:S(2)}, u32[]{:S(2)}) %collective-permute-start.29) | collective-permute-done | bytes 8224 | tf_op jit(solution)/shard_map/ppermute | solution.py:26
  138.6 1.4 pad_maximum_fusion.39
  140.7 14.2 %psum.15 = f32[2]{0:T(128)S(1)} all-reduce(f32[2]{0:T(128)S(1)} %pad_maximum_fusion.39), channel_id=1, replica_groups=mesh['cond'=4,'space'=8] {'space'}, use_global_device_ids=true, to_apply=%region_8.9 | all-reduce | flops 2 | bytes 16 | tf_op jit(solution)/shard_map/psum | solution.py:82
  (132 shorter events, 33.5 us)
Async XLA Ops:
  1.9 3.9 %collective-permute-start = (f32[2,2,1,2048]{3,2,0,1:T(1,128)S(1)}, f32[2,2,1,2048]{3,2,0,1:T(1,128)S(1)}, u32[]{:S(2)}, u32[]{:S(2)}) collective-permute-start(f32[2,2,1,2048]{3,2,0,1:T(1,128)S(1)} %get-tuple-element.99), channel_id=1, source_target_pairs={{0,1},{1,2},{2,3},{3,4},{4,5},{5,6},{6,7},{8,9},{9,10},{10,11},{11... | collective-permute-start | bytes 98312 | tf_op jit(solution)/shard_map/ppermute | solution.py:24
  4.4 5.3 %collective-permute-start.1 = (f32[2,2,1,2048]{3,2,0,1:T(1,128)S(1)}, f32[2,2,1,2048]{3,2,0,1:T(1,128)S(1)}, u32[]{:S(2)}, u32[]{:S(2)}) collective-permute-start(f32[2,2,1,2048]{3,2,0,1:T(1,128)S(1)} %get-tuple-element.100), channel_id=1, source_target_pairs={{1,0},{2,1},{3,2},{4,3},{5,4},{6,5},{7,6},{9,8},{10,9},{11,10},{12... | collective-permute-start | bytes 98312 | tf_op jit(solution)/shard_map/ppermute | solution.py:26
  11.8 5.8 %collective-permute-start.2 = (f32[2,2,1,2048]{3,2,0,1:T(1,128)S(1)}, f32[2,2,1,2048]{3,2,0,1:T(1,128)S(1)}, u32[]{:S(2)}, u32[]{:S(2)}) collective-permute-start(f32[2,2,1,2048]{3,2,0,1:T(1,128)S(1)} %get-tuple-element.97), channel_id=1, source_target_pairs={{0,1},{1,2},{2,3},{3,4},{4,5},{5,6},{6,7},{8,9},{9,10},{10,11},{11... | collective-permute-start | bytes 98312 | tf_op jit(solution)/shard_map/ppermute | solution.py:24
  16.3 3.1 %collective-permute-start.3 = (f32[2,2,1,2048]{3,2,0,1:T(1,128)S(1)}, f32[2,2,1,2048]{3,2,0,1:T(1,128)S(1)}, u32[]{:S(2)}, u32[]{:S(2)}) collective-permute-start(f32[2,2,1,2048]{3,2,0,1:T(1,128)S(1)} %get-tuple-element.98), channel_id=1, source_target_pairs={{1,0},{2,1},{3,2},{4,3},{5,4},{6,5},{7,6},{9,8},{10,9},{11,10},{12... | collective-permute-start | bytes 98312 | tf_op jit(solution)/shard_map/ppermute | solution.py:26
  20.3 5.4 %copy-start.6 = (s32[16,2048]{1,0:T(8,128)S(1)}, s32[16,2048]{1,0:T(8,128)}, u32[]{:S(2)}) copy-start(s32[16,2048]{1,0:T(8,128)} %param.12) | copy-start | bytes 393220
  20.4 5.4 %collective-permute-start.4 = (f32[2,2,1,2048]{3,2,0,1:T(1,128)S(1)}, f32[2,2,1,2048]{3,2,0,1:T(1,128)S(1)}, u32[]{:S(2)}, u32[]{:S(2)}) collective-permute-start(f32[2,2,1,2048]{3,2,0,1:T(1,128)S(1)} %get-tuple-element.95), channel_id=1, source_target_pairs={{0,1},{1,2},{2,3},{3,4},{4,5},{5,6},{6,7},{8,9},{9,10},{10,11},{11... | collective-permute-start | bytes 98312 | tf_op jit(solution)/shard_map/ppermute | solution.py:24
  24.4 3.1 %collective-permute-start.5 = (f32[2,2,1,2048]{3,2,0,1:T(1,128)S(1)}, f32[2,2,1,2048]{3,2,0,1:T(1,128)S(1)}, u32[]{:S(2)}, u32[]{:S(2)}) collective-permute-start(f32[2,2,1,2048]{3,2,0,1:T(1,128)S(1)} %get-tuple-element.96), channel_id=1, source_target_pairs={{1,0},{2,1},{3,2},{4,3},{5,4},{6,5},{7,6},{9,8},{10,9},{11,10},{12... | collective-permute-start | bytes 98312 | tf_op jit(solution)/shard_map/ppermute | solution.py:26
  28.6 5.4 %collective-permute-start.6 = (f32[2,2,1,2048]{3,2,0,1:T(1,128)S(1)}, f32[2,2,1,2048]{3,2,0,1:T(1,128)S(1)}, u32[]{:S(2)}, u32[]{:S(2)}) collective-permute-start(f32[2,2,1,2048]{3,2,0,1:T(1,128)S(1)} %get-tuple-element.93), channel_id=1, source_target_pairs={{0,1},{1,2},{2,3},{3,4},{4,5},{5,6},{6,7},{8,9},{9,10},{10,11},{11... | collective-permute-start | bytes 98312 | tf_op jit(solution)/shard_map/ppermute | solution.py:24
  32.7 3.1 %collective-permute-start.7 = (f32[2,2,1,2048]{3,2,0,1:T(1,128)S(1)}, f32[2,2,1,2048]{3,2,0,1:T(1,128)S(1)}, u32[]{:S(2)}, u32[]{:S(2)}) collective-permute-start(f32[2,2,1,2048]{3,2,0,1:T(1,128)S(1)} %get-tuple-element.94), channel_id=1, source_target_pairs={{1,0},{2,1},{3,2},{4,3},{5,4},{6,5},{7,6},{9,8},{10,9},{11,10},{12... | collective-permute-start | bytes 98312 | tf_op jit(solution)/shard_map/ppermute | solution.py:26
  37.0 5.4 %collective-permute-start.8 = (f32[2,2,1,2048]{3,2,0,1:T(1,128)S(1)}, f32[2,2,1,2048]{3,2,0,1:T(1,128)S(1)}, u32[]{:S(2)}, u32[]{:S(2)}) collective-permute-start(f32[2,2,1,2048]{3,2,0,1:T(1,128)S(1)} %get-tuple-element.91), channel_id=1, source_target_pairs={{0,1},{1,2},{2,3},{3,4},{4,5},{5,6},{6,7},{8,9},{9,10},{10,11},{11... | collective-permute-start | bytes 98312 | tf_op jit(solution)/shard_map/ppermute | solution.py:24
  41.1 3.1 %collective-permute-start.9 = (f32[2,2,1,2048]{3,2,0,1:T(1,128)S(1)}, f32[2,2,1,2048]{3,2,0,1:T(1,128)S(1)}, u32[]{:S(2)}, u32[]{:S(2)}) collective-permute-start(f32[2,2,1,2048]{3,2,0,1:T(1,128)S(1)} %get-tuple-element.92), channel_id=1, source_target_pairs={{1,0},{2,1},{3,2},{4,3},{5,4},{6,5},{7,6},{9,8},{10,9},{11,10},{12... | collective-permute-start | bytes 98312 | tf_op jit(solution)/shard_map/ppermute | solution.py:26
  45.5 10.4 %collective-permute-start.10 = (f32[2,2,1,2048]{3,2,0,1:T(1,128)S(1)}, f32[2,2,1,2048]{3,2,0,1:T(1,128)S(1)}, u32[]{:S(2)}, u32[]{:S(2)}) collective-permute-start(f32[2,2,1,2048]{3,2,0,1:T(1,128)S(1)} %get-tuple-element.89), channel_id=1, source_target_pairs={{0,1},{1,2},{2,3},{3,4},{4,5},{5,6},{6,7},{8,9},{9,10},{10,11},{11... | collective-permute-start | bytes 98312 | tf_op jit(solution)/shard_map/ppermute | solution.py:24
  49.6 6.3 %collective-permute-start.11 = (f32[2,2,1,2048]{3,2,0,1:T(1,128)S(1)}, f32[2,2,1,2048]{3,2,0,1:T(1,128)S(1)}, u32[]{:S(2)}, u32[]{:S(2)}) collective-permute-start(f32[2,2,1,2048]{3,2,0,1:T(1,128)S(1)} %get-tuple-element.90), channel_id=1, source_target_pairs={{1,0},{2,1},{3,2},{4,3},{5,4},{6,5},{7,6},{9,8},{10,9},{11,10},{12... | collective-permute-start | bytes 98312 | tf_op jit(solution)/shard_map/ppermute | solution.py:26
  50.9 26.5 %collective-permute-start.16 = (f32[2,1,2048]{2,1,0:T(1,128)S(1)}, f32[2,1,2048]{2,1,0:T(1,128)S(1)}, u32[]{:S(2)}, u32[]{:S(2)}) collective-permute-start(f32[2,1,2048]{2,1,0:T(1,128)S(1)} %get-tuple-element.101), channel_id=1, source_target_pairs={{1,0},{2,1},{3,2},{4,3},{5,4},{6,5},{7,6},{9,8},{10,9},{11,10},{12... | collective-permute-start | bytes 49160 | tf_op jit(solution)/shard_map/ppermute | solution.py:26
  52.2 29.5 %collective-permute-start.17 = (f32[2,1,2048]{2,1,0:T(1,128)S(1)}, f32[2,1,2048]{2,1,0:T(1,128)S(1)}, u32[]{:S(2)}, u32[]{:S(2)}) collective-permute-start(f32[2,1,2048]{2,1,0:T(1,128)S(1)} %get-tuple-element.102), channel_id=1, source_target_pairs={{0,1},{1,2},{2,3},{3,4},{4,5},{5,6},{6,7},{8,9},{9,10},{10,11},{11... | collective-permute-start | bytes 49160 | tf_op jit(solution)/shard_map/ppermute | solution.py:24
  57.3 6.3 %collective-permute-start.12 = (f32[2,2,1,2048]{3,2,0,1:T(1,128)S(1)}, f32[2,2,1,2048]{3,2,0,1:T(1,128)S(1)}, u32[]{:S(2)}, u32[]{:S(2)}) collective-permute-start(f32[2,2,1,2048]{3,2,0,1:T(1,128)S(1)} %get-tuple-element.87), channel_id=1, source_target_pairs={{0,1},{1,2},{2,3},{3,4},{4,5},{5,6},{6,7},{8,9},{9,10},{10,11},{11... | collective-permute-start | bytes 98312 | tf_op jit(solution)/shard_map/ppermute | solution.py:24
  61.0 3.1 %collective-permute-start.13 = (f32[2,2,1,2048]{3,2,0,1:T(1,128)S(1)}, f32[2,2,1,2048]{3,2,0,1:T(1,128)S(1)}, u32[]{:S(2)}, u32[]{:S(2)}) collective-permute-start(f32[2,2,1,2048]{3,2,0,1:T(1,128)S(1)} %get-tuple-element.88), channel_id=1, source_target_pairs={{1,0},{2,1},{3,2},{4,3},{5,4},{6,5},{7,6},{9,8},{10,9},{11,10},{12... | collective-permute-start | bytes 98312 | tf_op jit(solution)/shard_map/ppermute | solution.py:26
  62.3 20.7 %collective-permute-start.18 = (f32[2,1,2048]{2,1,0:T(1,128)S(1)}, f32[2,1,2048]{2,1,0:T(1,128)S(1)}, u32[]{:S(2)}, u32[]{:S(2)}) collective-permute-start(f32[2,1,2048]{2,1,0:T(1,128)S(1)} %get-tuple-element.103), channel_id=1, source_target_pairs={{1,0},{2,1},{3,2},{4,3},{5,4},{6,5},{7,6},{9,8},{10,9},{11,10},{12... | collective-permute-start | bytes 49160 | tf_op jit(solution)/shard_map/ppermute | solution.py:26
  65.6 5.4 %collective-permute-start.14 = (f32[2,2,1,2048]{3,2,0,1:T(1,128)S(1)}, f32[2,2,1,2048]{3,2,0,1:T(1,128)S(1)}, u32[]{:S(2)}, u32[]{:S(2)}) collective-permute-start(f32[2,2,1,2048]{3,2,0,1:T(1,128)S(1)} %get-tuple-element.85), channel_id=1, source_target_pairs={{0,1},{1,2},{2,3},{3,4},{4,5},{5,6},{6,7},{8,9},{9,10},{10,11},{11... | collective-permute-start | bytes 98312 | tf_op jit(solution)/shard_map/ppermute | solution.py:24
  69.6 4.8 %collective-permute-start.15 = (f32[2,2,1,2048]{3,2,0,1:T(1,128)S(1)}, f32[2,2,1,2048]{3,2,0,1:T(1,128)S(1)}, u32[]{:S(2)}, u32[]{:S(2)}) collective-permute-start(f32[2,2,1,2048]{3,2,0,1:T(1,128)S(1)} %get-tuple-element.86), channel_id=1, source_target_pairs={{1,0},{2,1},{3,2},{4,3},{5,4},{6,5},{7,6},{9,8},{10,9},{11,10},{12... | collective-permute-start | bytes 98312 | tf_op jit(solution)/shard_map/ppermute | solution.py:26
  71.0 17.0 %collective-permute-start.19 = (f32[2,1,2048]{2,1,0:T(1,128)S(1)}, f32[2,1,2048]{2,1,0:T(1,128)S(1)}, u32[]{:S(2)}, u32[]{:S(2)}) collective-permute-start(f32[2,1,2048]{2,1,0:T(1,128)S(1)} %get-tuple-element.104), channel_id=1, source_target_pairs={{0,1},{1,2},{2,3},{3,4},{4,5},{5,6},{6,7},{8,9},{9,10},{10,11},{11... | collective-permute-start | bytes 49160 | tf_op jit(solution)/shard_map/ppermute | solution.py:24
  74.4 17.2 %collective-permute-start.20 = (f32[2,1,2048]{2,1,0:T(1,128)S(1)}, f32[2,1,2048]{2,1,0:T(1,128)S(1)}, u32[]{:S(2)}, u32[]{:S(2)}) collective-permute-start(f32[2,1,2048]{2,1,0:T(1,128)S(1)} %get-tuple-element.105), channel_id=1, source_target_pairs={{1,0},{2,1},{3,2},{4,3},{5,4},{6,5},{7,6},{9,8},{10,9},{11,10},{12... | collective-permute-start | bytes 49160 | tf_op jit(solution)/shard_map/ppermute | solution.py:26
  77.4 15.7 %collective-permute-start.21 = (f32[2,1,2048]{2,1,0:T(1,128)S(1)}, f32[2,1,2048]{2,1,0:T(1,128)S(1)}, u32[]{:S(2)}, u32[]{:S(2)}) collective-permute-start(f32[2,1,2048]{2,1,0:T(1,128)S(1)} %get-tuple-element.106), channel_id=1, source_target_pairs={{0,1},{1,2},{2,3},{3,4},{4,5},{5,6},{6,7},{8,9},{9,10},{10,11},{11... | collective-permute-start | bytes 49160 | tf_op jit(solution)/shard_map/ppermute | solution.py:24
  81.7 5.6 %copy-start.7 = (s32[8]{0:T(128)S(1)}, s32[8]{0:T(128)}, u32[]{:S(2)}) copy-start(s32[8]{0:T(128)} %param.13) | copy-start | bytes 100
  81.7 11.4 %collective-permute-start.22 = (f32[2,1,2048]{2,1,0:T(1,128)S(1)}, f32[2,1,2048]{2,1,0:T(1,128)S(1)}, u32[]{:S(2)}, u32[]{:S(2)}) collective-permute-start(f32[2,1,2048]{2,1,0:T(1,128)S(1)} %get-tuple-element.107), channel_id=1, source_target_pairs={{1,0},{2,1},{3,2},{4,3},{5,4},{6,5},{7,6},{9,8},{10,9},{11,10},{12... | collective-permute-start | bytes 49160 | tf_op jit(solution)/shard_map/ppermute | solution.py:26
  83.0 10.1 %collective-permute-start.23 = (f32[2,1,2048]{2,1,0:T(1,128)S(1)}, f32[2,1,2048]{2,1,0:T(1,128)S(1)}, u32[]{:S(2)}, u32[]{:S(2)}) collective-permute-start(f32[2,1,2048]{2,1,0:T(1,128)S(1)} %get-tuple-element.108), channel_id=1, source_target_pairs={{0,1},{1,2},{2,3},{3,4},{4,5},{5,6},{6,7},{8,9},{9,10},{10,11},{11... | collective-permute-start | bytes 49160 | tf_op jit(solution)/shard_map/ppermute | solution.py:24
  88.0 21.6 %collective-permute-start.24 = (f32[1,2048]{1,0:T(1,128)S(1)}, f32[1,2048]{1,0:T(1,128)S(1)}, u32[]{:S(2)}, u32[]{:S(2)}) collective-permute-start(f32[1,2048]{1,0:T(1,128)S(1)} %get-tuple-element.111), channel_id=1, source_target_pairs={{0,1},{1,2},{2,3},{3,4},{4,5},{5,6},{6,7},{8,9},{9,10},{10,11},{11... | collective-permute-start | bytes 24584 | tf_op jit(solution)/shard_map/ppermute | solution.py:24
  91.7 17.9 %collective-permute-start.26 = (f32[1,2048]{1,0:T(1,128)S(1)}, f32[1,2048]{1,0:T(1,128)S(1)}, u32[]{:S(2)}, u32[]{:S(2)}) collective-permute-start(f32[1,2048]{1,0:T(1,128)S(1)} %get-tuple-element.112), channel_id=1, source_target_pairs={{1,0},{2,1},{3,2},{4,3},{5,4},{6,5},{7,6},{9,8},{10,9},{11,10},{12... | collective-permute-start | bytes 24584 | tf_op jit(solution)/shard_map/ppermute | solution.py:26
  106.8 2.9 %collective-permute-start.25 = (f32[1,2048]{1,0:T(1,128)S(1)}, f32[1,2048]{1,0:T(1,128)S(1)}, u32[]{:S(2)}, u32[]{:S(2)}) collective-permute-start(f32[1,2048]{1,0:T(1,128)S(1)} %get-tuple-element.113), channel_id=1, source_target_pairs={{0,1},{1,2},{2,3},{3,4},{4,5},{5,6},{6,7},{8,9},{9,10},{10,11},{11... | collective-permute-start | bytes 24584 | tf_op jit(solution)/shard_map/ppermute | solution.py:24
  108.3 4.5 %collective-permute-start.27 = (f32[1,2048]{1,0:T(1,128)S(1)}, f32[1,2048]{1,0:T(1,128)S(1)}, u32[]{:S(2)}, u32[]{:S(2)}) collective-permute-start(f32[1,2048]{1,0:T(1,128)S(1)} %get-tuple-element.114), channel_id=1, source_target_pairs={{1,0},{2,1},{3,2},{4,3},{5,4},{6,5},{7,6},{9,8},{10,9},{11,10},{12... | collective-permute-start | bytes 24584 | tf_op jit(solution)/shard_map/ppermute | solution.py:26
  133.1 2.6 %collective-permute-start.28 = (f32[1,2048]{1,0:T(1,128)S(1)}, f32[1,2048]{1,0:T(1,128)S(1)}, u32[]{:S(2)}, u32[]{:S(2)}) collective-permute-start(f32[1,2048]{1,0:T(1,128)S(1)} %get-tuple-element.109), channel_id=1, source_target_pairs={{0,1},{1,2},{2,3},{3,4},{4,5},{5,6},{6,7},{8,9},{9,10},{10,11},{11... | collective-permute-start | bytes 24584 | tf_op jit(solution)/shard_map/ppermute | solution.py:24
  134.4 3.1 %collective-permute-start.29 = (f32[1,2048]{1,0:T(1,128)S(1)}, f32[1,2048]{1,0:T(1,128)S(1)}, u32[]{:S(2)}, u32[]{:S(2)}) collective-permute-start(f32[1,2048]{1,0:T(1,128)S(1)} %get-tuple-element.110), channel_id=1, source_target_pairs={{1,0},{2,1},{3,2},{4,3},{5,4},{6,5},{7,6},{9,8},{10,9},{11,10},{12... | collective-permute-start | bytes 24584 | tf_op jit(solution)/shard_map/ppermute | solution.py:26
  (6 other events, 13.9 us)
